TPU v7x, 512 devices: a whole 4x4x16 slice. The times are simulated.
512 devices in a mesh: fsdp: 128 (over y, z_lo, x), dp: 4 (over z_hi, core).
Axes of the slice: x: 4, y: 4, z: 16 (z_hi: 2, z_lo: 8; z = z_hi * 8 + z_lo), core: 2. Of those that a mesh axis runs over, the one named last changes fastest.
Arguments:
- tokens: bfloat16 [65536, 4096], P(('fsdp', 'dp')), may hold values from -6 to 6
- norm_gain: float32 [4096], replicated, may hold values from 0.25 to 1.75
- penalty: float32 [14336], P('dp'), may hold values from 0.25 to 4
- weight_tiles: bfloat16 [4, 384, 4096], P(None, 'fsdp'), may hold values from -0.375 to 0.375
- block_rows: int32 [224, 4], replicated, may hold values from 0 to 63, as said below
- block_slot: int32 [224, 4], replicated, may hold values from 0 to 383, as said below
Outputs:
- grad_tokens: bfloat16 [65536, 4096], P(('fsdp', 'dp'))
Inputs may be any that keep to these rules, and one draw needn't show every extreme that they name: `block_rows`: each block column names 4 distinct block rows. Within each run of 56 block columns (columns q * 56 to (q + 1) * 56 - 1), a block row is named at most 4 times, and some block row exactly 4 times. `block_slot`: within each run of 56 block columns, no slot is named twice. Slot s is stored by fsdp index s // 3; in each run some fsdp index has all 3 of its slots named.
All inputs are finite; a program needn't handle non-finite values.
Results may differ from a plain program's by a relative error of at most 0.014.
Values may be sent and summed in bfloat16 or wider, within the bound.
No kernel may reach another device: no remote copies, remote signals or barrier semaphores. Data moves between devices by JAX's collectives and lax.ppermute only.
A program may use at most 128 MiB of HBM per device.

v0:
```python
import math
import jax
import jax.numpy as jnp
from jax import lax
from jax.sharding import PartitionSpec as P

BLOCK = 64


def on_device(tokens, norm_gain, penalty, weight_tiles, block_rows, block_slot):
    quarter = lax.axis_index("dp")
    model_width = tokens.shape[1]
    as_float = tokens.astype(jnp.float32)
    rms_scale = jnp.sqrt(jnp.mean(as_float * as_float, axis=1, keepdims=True) + 1e-05)
    normed = as_float / rms_scale
    scaled = (normed * norm_gain).astype(jnp.bfloat16)
    own_tiles = lax.dynamic_index_in_dim(weight_tiles, quarter, 0, keepdims=False)
    gathered = lax.all_gather(scaled, "dp", axis=0, tiled=True)
    group_rows = gathered.shape[0]
    row_blocks = model_width // BLOCK
    per_column = block_rows.shape[1]
    col_blocks = penalty.shape[0] // BLOCK
    rows_here = lax.dynamic_slice_in_dim(block_rows, quarter * col_blocks, col_blocks, 0)
    slots_here = lax.dynamic_slice_in_dim(block_slot, quarter * col_blocks, col_blocks, 0)
    entries = col_blocks * per_column
    flat_slots = slots_here.reshape(-1)
    stored = lax.all_gather(own_tiles, "fsdp", axis=0, tiled=True)
    weights_here = stored[flat_slots].reshape(entries, BLOCK, BLOCK)
    feat_blocks = gathered.T.reshape(row_blocks, BLOCK, group_rows)
    unit_scale = penalty.reshape(col_blocks, BLOCK, 1)
    col_size = math.gcd(col_blocks, 4)
    col_groups = col_blocks // col_size

    def forward_group(pieces):
        weight_group, row_group, unit_group = pieces
        selected = feat_blocks[row_group]
        preact = jnp.einsum(
            "gkio,gkin->gon", weight_group, selected, preferred_element_type=jnp.float32
        )
        gating = jax.nn.sigmoid(preact)
        grad_act = unit_group * (preact * gating)
        grad_pre = grad_act * (gating * (1.0 + preact * (1.0 - gating)))
        return grad_pre.astype(jnp.bfloat16)

    grad_pre = lax.map(
        forward_group,
        (
            weights_here.reshape(col_groups, col_size, per_column, BLOCK, BLOCK),
            rows_here.reshape(col_groups, col_size, per_column),
            unit_scale.reshape(col_groups, col_size, BLOCK, 1),
        ),
    )
    grad_pre = grad_pre.reshape(col_blocks, BLOCK, group_rows)
    row_cap = -(-entries // row_blocks)
    flat_rows = rows_here.reshape(-1)
    row_hits = (flat_rows[:, None] == jnp.arange(row_blocks, dtype=jnp.int32)[None, :]).astype(
        jnp.int32
    )
    hits_before = jnp.cumsum(row_hits, axis=0) - row_hits
    row_rank = jnp.sum(hits_before * row_hits, axis=1)
    slot_table = jnp.full((row_blocks * row_cap,), entries, jnp.int32)
    slot_table = slot_table.at[flat_rows * row_cap + row_rank].set(
        jnp.arange(entries, dtype=jnp.int32)
    )
    padded_tiles = jnp.concatenate([weights_here, jnp.zeros((1, BLOCK, BLOCK), jnp.bfloat16)], 0)
    back_tiles = padded_tiles[slot_table].reshape(row_blocks, row_cap, BLOCK, BLOCK)
    back_columns = jnp.where(slot_table < entries, slot_table // per_column, 0).reshape(
        row_blocks, row_cap
    )
    row_size = math.gcd(row_blocks, 4)
    row_groups = row_blocks // row_size
    grad_part = grad_pre

    def one_group(pieces):
        tile_group, column_group = pieces
        selected = grad_part[column_group]
        return jnp.einsum(
            "gqio,gqon->ngi", tile_group, selected, preferred_element_type=jnp.float32
        )

    grouped = lax.map(
        one_group,
        (
            back_tiles.reshape(row_groups, row_size, row_cap, BLOCK, BLOCK),
            back_columns.reshape(row_groups, row_size, row_cap),
        ),
    )
    summed = lax.psum_scatter(
        grouped.transpose(1, 0, 2, 3).reshape(group_rows, model_width).astype(jnp.bfloat16),
        "dp",
        scatter_dimension=0,
        tiled=True,
    ).astype(jnp.float32)
    grad_norm = summed * norm_gain
    mixing = jnp.mean(grad_norm * normed, axis=1, keepdims=True)
    return ((grad_norm - normed * mixing) / rms_scale).astype(jnp.bfloat16)


def solution(mesh):
    placed = (P(("fsdp", "dp"), None), P(), P("dp"), P(None, "fsdp", None), P(), P())
    return jax.shard_map(
        on_device, mesh=mesh, in_specs=placed, out_specs=P(("fsdp", "dp"), None), check_vma=False
    )
```

profile of v0, /device:TPU:1, one launch (start us, length us, event | category | flops | bytes accessed | tf_op | source)
XLA Modules:
  0.0 1400.3 jit_solution(17715397416254381017)
XLA Ops:
  10.4 2.2 multiply_convert_fusion.1
  16.2 877.6 %all-gather.6.cloned.1.call-done = bf16[1,384,4096]{2,0,1:T(2,128)(2,1)} async-done(((bf16[1,3,4096]{2,0,1:T(2,128)(2,1)}), bf16[1,384,4096]{2,0,1:T(2,128)(2,1)}) %all-gather.6.cloned.1.call-update) | async-done | bytes 3145744 | tf_op jit(solution)/shard_map/all_gather | solution.py:27
  893.8 6.3 copy.69
  900.2 2.9 gather_fusion.2
  903.1 4.1 copy.55
  907.2 4.9 reshape_reshape.14
  912.1 5.6 copy.56
  917.8 4.9 concatenate.3
  922.6 5.1 gather_fusion.3
  927.7 174.2 %all-gather.4.cloned.1.call-done = bf16[512,4096]{0,1:T(8,128)(2,1)} async-done(((bf16[128,4096]{0,1:T(8,128)(2,1)}), bf16[512,4096]{0,1:T(8,128)(2,1)}) %all-gather.4.cloned.1.call-update) | async-done | bytes 4194320 | tf_op jit(solution)/shard_map/all_gather | solution.py:18
  1101.9 70.7 %while.20 = (s32[]{:T(128)}, bf16[14,4,64,512]{3,2,1,0:T(8,128)(2,1)}, f32[14,4,64,1]{2,1,3,0:T(4,128)S(1)}, bf16[14,4,4,64,64]{4,3,2,1,0:T(8,128)(2,1)}, s32[14...) while((s32[]{:T(128)}, bf16[14,4,64,512]{3,2,1,0:T(8,128)(2,1)}, ...), condition=%wide.region_6.7_spmd, body=%wide.region_5.6_spmd.sunk | while | flops 68551728 | bytes 3678677 | solution.py:45
  1102.0 2.8 gather_fusion
  1104.9 2.1 fusion.24
  1107.1 2.8 gather_fusion
  1112.2 2.8 gather_fusion
  1117.2 2.8 gather_fusion
  1122.3 2.8 gather_fusion
  1127.3 2.8 gather_fusion
  1132.3 2.8 gather_fusion
  1135.2 2.1 fusion.24
  1137.4 2.8 gather_fusion
  1142.4 2.8 gather_fusion
  1147.5 2.8 gather_fusion
  1152.5 2.8 gather_fusion
  1157.5 2.8 gather_fusion
  1160.4 2.1 fusion.24
  1162.6 2.8 gather_fusion
  1165.4 2.1 fusion.24
  1167.7 2.8 gather_fusion
  1172.6 76.2 %while.21 = (s32[]{:T(128)}, bf16[16,512,4,64]{1,3,2,0:T(8,128)(2,1)}, s32[16,4,4]{2,1,0:T(4,128)S(1)}, bf16[56,64,512]{2,1,0:T(8,128)(2,1)}, bf16[16,4,4,64,64]{4,3,2,1,0:T(8,128)(2,1)}, /*index=5*/s32[]{:T(128)}) while((s32[]{:T(128)}, bf16[16,512,4,64]{1,3,2,0:T(8,128)(2,1)}, s32[16,4,4]{2,1,0:T(4,128)S(1)}, ...), condition=%wide.region_8.9_spmd, body=%wide.region_7.8_spmd.sunk | while | flops 67109936 | bytes 3937737 | solution.py:81
  1172.7 2.7 gather_fusion.1
  1177.5 2.7 gather_fusion.1
  1182.2 2.7 gather_fusion.1
  1187.0 2.7 gather_fusion.1
  1191.8 2.7 gather_fusion.1
  1196.5 2.7 gather_fusion.1
  1201.3 2.7 gather_fusion.1
  1206.0 2.7 gather_fusion.1
  1210.8 2.7 gather_fusion.1
  1215.5 2.7 gather_fusion.1
  1220.3 2.7 gather_fusion.1
  1225.1 2.7 gather_fusion.1
  1229.8 2.7 gather_fusion.1
  1234.6 2.7 gather_fusion.1
  1239.4 2.7 gather_fusion.1
  1244.1 2.7 gather_fusion.1
  1248.8 6.4 copy.60
  1255.3 134.1 %reduce-scatter.4.cloned.1.call-done = bf16[128,4096]{1,0:T(8,128)(2,1)} async-done(((bf16[512,4096]{1,0:T(8,128)(2,1)}), bf16[128,4096]{1,0:T(8,128)(2,1)}) %reduce-scatter.4.cloned.1.call-update) | async-done | bytes 1048592
  (187 shorter events, 68.0 us)
Async XLA Ops:
  6.5 0.9 copy-start
  6.5 6.1 copy-start.6
  6.5 7.5 copy-start.7
  6.5 7.8 copy-start.5
  6.5 887.3 %all-gather.6.cloned.1.call-start = ((), (), s32[]{:S(2)}) async-start(), calls=%async_computation.2 | async-start | bytes 6340608 | tf_op jit(solution)/shard_map/all_gather | solution.py:27
  8.1 1093.8 %all-gather.4.cloned.1.call-start = ((), (), s32[]{:S(2)}) async-start(), calls=%async_computation.1 | async-start | bytes 5242880 | tf_op jit(solution)/shard_map/all_gather | solution.py:18
  9.8 6.4 copy-start.1
  12.6 1376.8 %reduce-scatter.4.cloned.1.call-start = ((), (), s32[]{:S(2)}) async-start(), calls=%async_computation.3 | async-start | bytes 5242880
  903.1 4.1 copy-start.3
  1255.2 135.8 %copy-start.2 = (bf16[128,4096]{0,1:T(8,128)(2,1)S(1)}, bf16[128,4096]{0,1:T(8,128)(2,1)}, u32[]{:S(2)}) copy-start(bf16[128,4096]{0,1:T(8,128)(2,1)} %copy-done.1) | copy-start | bytes 3145732
  1255.2 135.8 %copy-start.4 = (f32[4096]{0:T(1024)S(1)}, f32[4096]{0:T(1024)}, u32[]{:S(2)}) copy-start(f32[4096]{0:T(1024)} %param.11) | copy-start | bytes 49156
Sparse Core Ops, SparseCore 0:
  9.4 884.3 all-gather.5
  895.9 205.9 all-gather.3
  1255.4 133.9 reduce-scatter.3
where the time goes:
time: 1400 us
  waiting for transfers between devices  1190 us (85%)
  local copies, waits for them, and re-layouts  133 us (10%)
  matrix products  61.8 us (4%)
    all_gather x1, waiting for transfers between devices, on_device(): stored = lax.all_gather(own_tiles, 'fsdp', axis=0, tiled=True)  878 us
    all_gather x1, waiting for transfers between devices, on_device(): gathered = lax.all_gather(scaled, 'dp', axis=0, tiled=True)  174 us
    unnamed x4, waiting for transfers between devices  134 us
    gather x16, local copies, waits for them, and re-layouts, one_group(): selected = grad_part[column_group]  42.4 us
    gather x14, local copies, waits for them, and re-layouts, forward_group(): selected = feat_blocks[row_group]  39.2 us
    dot_general x16, matrix products, one_group(): jnp.einsum('gqio,gqon->ngi', tile_group, selected, preferred_element_type...  32.1 us
    dot_general x14, matrix products, forward_group(): jnp.einsum('gkio,gkin->gon', weight_group, selected, preferred_element_ty...  29.7 us
  transfers between devices with their start and end apart: 3, of which 3 were waited for; matrix products, arithmetic and copies ran while one was open for 3% of the time, Pallas kernels for 0%

commit v1 on v0

--- a/solution.py
+++ b/solution.py
@@ -24,7 +24,12 @@
     slots_here = lax.dynamic_slice_in_dim(block_slot, quarter * col_blocks, col_blocks, 0)
     entries = col_blocks * per_column
     flat_slots = slots_here.reshape(-1)
-    stored = lax.all_gather(own_tiles, "fsdp", axis=0, tiled=True)
+    stored = jnp.concatenate(
+        lax.all_to_all(
+            jnp.stack(tuple((own_tiles for _ in range(lax.axis_size("fsdp"))))), "fsdp", 0, 0
+        ),
+        axis=0,
+    )
     weights_here = stored[flat_slots].reshape(entries, BLOCK, BLOCK)
     feat_blocks = gathered.T.reshape(row_blocks, BLOCK, group_rows)
     unit_scale = penalty.reshape(col_blocks, BLOCK, 1)

time: 1400 us -> 648 us (0.46)
  waiting for transfers between devices: 1190 us -> 408 us
  starting transfers between devices: 0.12 us -> 21.1 us
    all_gather x1 -> x0, waiting for transfers between devices: 878 us -> none  [on_device(): stored = lax.all_gather(own_tiles, 'fsdp', axis=0, tiled=True)]
    all_to_all x0 -> x1, waiting for transfers between devices: none -> 267 us  [on_device(): lax.all_to_all(jnp.stack(tuple((own_tiles for _ in range(lax.axis_size('f...]
    all_gather x1, waiting for transfers between devices: 174 us -> 0.01 us  [on_device(): gathered = lax.all_gather(scaled, 'dp', axis=0, tiled=True)]
    all_to_all x0 -> x1, starting transfers between devices: none -> 21.1 us  [on_device(): lax.all_to_all(jnp.stack(tuple((own_tiles for _ in range(lax.axis_size('f...]
    unnamed x4 -> x3, waiting for transfers between devices: 134 us -> 141 us
  transfers between devices with their start and end apart: 3 -> 3, of which waited for: 3 -> 2; matrix products, arithmetic and copies ran while one was open for 3% -> 5% of each run, Pallas kernels for 0% -> 0%
where the time goes in v1:
time: 648 us; the launch traced here: 645 us
  waiting for transfers between devices  408 us (63%)
  local copies, waits for them, and re-layouts  136 us (21%)
  matrix products  61.8 us (10%)
  starting transfers between devices  21.1 us (3%)
  between operations  13.7 us (2%)
    all_to_all x1, waiting for transfers between devices, on_device(): lax.all_to_all(jnp.stack(tuple((own_tiles for _ in range(lax.axis_size('f...  267 us
    unnamed x3, waiting for transfers between devices  141 us
    gather x16, local copies, waits for them, and re-layouts, one_group(): selected = grad_part[column_group]  42.4 us
    gather x14, local copies, waits for them, and re-layouts, forward_group(): selected = feat_blocks[row_group]  39.2 us
    dot_general x16, matrix products, one_group(): jnp.einsum('gqio,gqon->ngi', tile_group, selected, preferred_element_type...  32.1 us
    dot_general x14, matrix products, forward_group(): jnp.einsum('gkio,gkin->gon', weight_group, selected, preferred_element_ty...  29.7 us
    all_to_all x1, starting transfers between devices, on_device(): lax.all_to_all(jnp.stack(tuple((own_tiles for _ in range(lax.axis_size('f...  21.1 us
  transfers between devices with their start and end apart: 3, of which 2 were waited for; matrix products, arithmetic and copies ran while one was open for 5% of the time, Pallas kernels for 0%

profile of v1, /device:TPU:1, one launch (start us, length us, event | category | flops | bytes accessed | tf_op | source)
XLA Modules:
  0.0 645.5 jit_solution(2716023402803928321)
XLA Ops:
  7.5 4.0 stack.2
  11.6 21.1 %all-to-all-start = ((bf16[128,3,4096]{2,1,0:T(4,128)(2,1)}), bf16[128,3,4096]{2,1,0:T(4,128)(2,1)}, u32[]{:S(2)}, u32[]{:S(2)}) async-start(bf16[128,3,4096]{2,1,0:T(4,128)(2,1)} %stack.2), calls=%async_computation | async-start | bytes 8388608 | tf_op jit(solution)/shard_map/all_to_all | solution.py:28
  39.1 267.2 %all-to-all-done = bf16[128,3,4096]{2,1,0:T(4,128)(2,1)} async-done(((bf16[128,3,4096]{2,1,0:T(4,128)(2,1)}), bf16[128,3,4096]{2,1,0:T(4,128)(2,1)}, u32[]{:S(2)}, u32[]{:S(2)}) %all-to-all-start) | async-done | bytes 3145760 | tf_op jit(solution)/shard_map/all_to_all | solution.py:28
  306.4 6.0 reshape.162
  312.3 2.9 gather_fusion.2
  315.3 4.1 copy.41
  319.4 4.9 reshape_reshape.14
  324.3 5.6 copy.42
  329.9 70.7 %while.20 = (s32[]{:T(128)}, bf16[14,4,64,512]{3,2,1,0:T(8,128)(2,1)}, f32[14,4,64,1]{2,1,3,0:T(4,128)S(1)}, bf16[14,4,4,64,64]{4,3,2,1,0:T(8,128)(2,1)}, s32[14...) while((s32[]{:T(128)}, bf16[14,4,64,512]{3,2,1,0:T(8,128)(2,1)}, ...), condition=%wide.region_6.7_spmd, body=%wide.region_5.6_spmd.sunk | while | flops 68551728 | bytes 3678677 | solution.py:50
  330.0 2.8 gather_fusion
  335.1 2.8 gather_fusion
  340.1 2.8 gather_fusion
  342.9 2.1 fusion.24
  345.2 2.8 gather_fusion
  350.2 2.8 gather_fusion
  355.3 2.8 gather_fusion
  360.3 2.8 gather_fusion
  363.2 2.1 fusion.24
  365.4 2.8 gather_fusion
  370.4 2.8 gather_fusion
  375.5 2.8 gather_fusion
  380.5 2.8 gather_fusion
  385.5 2.8 gather_fusion
  388.4 2.1 fusion.24
  390.6 2.8 gather_fusion
  393.4 2.1 fusion.24
  395.7 2.8 gather_fusion
  400.6 4.9 concatenate.3
  405.5 5.1 gather_fusion.3
  410.6 76.2 %while.21 = (s32[]{:T(128)}, bf16[16,512,4,64]{1,3,2,0:T(8,128)(2,1)}, s32[16,4,4]{2,1,0:T(4,128)S(1)}, bf16[56,64,512]{2,1,0:T(8,128)(2,1)}, bf16[16,4,4,64,64]{4,3,2,1,0:T(8,128)(2,1)}, /*index=5*/s32[]{:T(128)}) while((s32[]{:T(128)}, bf16[16,512,4,64]{1,3,2,0:T(8,128)(2,1)}, s32[16,4,4]{2,1,0:T(4,128)S(1)}, ...), condition=%wide.region_8.9_spmd, body=%wide.region_7.8_spmd.sunk | while | flops 67109936 | bytes 3937737 | solution.py:86
  410.7 2.7 gather_fusion.1
  415.5 2.7 gather_fusion.1
  420.2 2.7 gather_fusion.1
  425.0 2.7 gather_fusion.1
  429.8 2.7 gather_fusion.1
  434.5 2.7 gather_fusion.1
  439.3 2.7 gather_fusion.1
  444.1 2.7 gather_fusion.1
  448.9 2.7 gather_fusion.1
  453.6 2.7 gather_fusion.1
  458.4 2.7 gather_fusion.1
  463.1 2.7 gather_fusion.1
  467.9 2.7 gather_fusion.1
  472.6 2.7 gather_fusion.1
  477.4 2.7 gather_fusion.1
  482.2 2.7 gather_fusion.1
  486.8 6.5 %copy.46 = bf16[512,4096]{1,0:T(8,128)(2,1)} copy(bf16[512,4096]{0,1:T(8,128)(2,1)} %bitcast.102) | data formatting | bytes 8388608
  493.3 140.9 %reduce-scatter.4.cloned.1.call-done = bf16[128,4096]{1,0:T(8,128)(2,1)} async-done(((bf16[512,4096]{1,0:T(8,128)(2,1)}), bf16[128,4096]{1,0:T(8,128)(2,1)}) %reduce-scatter.4.cloned.1.call-update) | async-done | bytes 1048592
  (190 shorter events, 68.0 us)
Async XLA Ops:
  6.5 0.9 copy-start
  11.6 21.1 %copy-start.4 = (bf16[128,4096]{1,0:T(8,128)(2,1)S(1)}, bf16[128,4096]{1,0:T(8,128)(2,1)}, u32[]{:S(2)}) copy-start(bf16[128,4096]{1,0:T(8,128)(2,1)} %param.10) | copy-start | bytes 3145732
  11.6 22.4 %copy-start.5 = (f32[4096]{0:T(1024)S(1)}, f32[4096]{0:T(1024)}, u32[]{:S(2)}) copy-start(f32[4096]{0:T(1024)} %param.11) | copy-start | bytes 49156
  11.6 294.8 %all-to-all-start = ((bf16[128,3,4096]{2,1,0:T(4,128)(2,1)}), bf16[128,3,4096]{2,1,0:T(4,128)(2,1)}, u32[]{:S(2)}, u32[]{:S(2)}) async-start(bf16[128,3,4096]{2,1,0:T(4,128)(2,1)} %stack.2), calls=%async_computation | async-start | bytes 8388608 | tf_op jit(solution)/shard_map/all_to_all | solution.py:28
  32.6 2.9 copy-start.7
  32.7 4.3 copy-start.8
  32.7 4.6 copy-start.6
  32.7 297.2 %all-gather.2.cloned.1.call-start = ((), (), s32[]{:S(2)}) async-start(), calls=%async_computation.2 | async-start | bytes 5242880 | tf_op jit(solution)/shard_map/all_gather | solution.py:18
  33.4 5.7 copy-start.1
  35.5 598.7 %reduce-scatter.4.cloned.1.call-start = ((), (), s32[]{:S(2)}) async-start(), calls=%async_computation.3 | async-start | bytes 5242880
  315.3 4.1 copy-start.3
  493.3 142.6 %copy-start.2 = (bf16[128,4096]{0,1:T(8,128)(2,1)S(1)}, bf16[128,4096]{0,1:T(8,128)(2,1)}, u32[]{:S(2)}) copy-start(bf16[128,4096]{0,1:T(8,128)(2,1)} %copy-done.1) | copy-start | bytes 3145732
Sparse Core Ops, SparseCore 0:
  35.6 108.6 all-gather.1
  493.5 140.7 reduce-scatter.3
